TPU v7x, 32 devices: a whole 2x2x4 slice. The times are simulated.
32 devices in a mesh: grp: 2 (over y), row: 4 (over x, core), col: 4 (over z).
Axes of the slice: x: 2, y: 2, z: 4, core: 2. Of those that a mesh axis runs over, the one named last changes fastest.
Arguments:
- programs: bfloat16 [2048, 2048], P(('grp', 'row'), 'col'), parts along dimension 0, may hold values from -6 to 6
- tests: bfloat16 [2048, 2048], P(('grp', 'col'), 'row'), parts along dimension 0, may hold values from -6 to 6
- weight: bfloat16 [2048, 2048], P('col', 'row'), may hold values from -0.125 to 0.125
- labels: int32 [2048, 1024], P(('grp', 'row'), 'col'), parts along dimension 0, may hold values 0 or 1
Outputs:
- grad_programs: bfloat16 [2048, 2048], P(('grp', 'row'), 'col'), parts along dimension 0
- grad_tests: bfloat16 [2048, 2048], P(('grp', 'col'), 'row'), parts along dimension 0
- grad_weight: float32 [4096, 2048], P(('grp', 'col'), 'row'), parts along dimension 0
There are 2 independent parts, one for each index of `grp`. A program takes and returns all parts, laid end to end along the dimension named above; an argument that names none is the same for every part. Nothing has to cross between parts.
All inputs are finite; a program needn't handle non-finite values. No bound on the sum of `labels` on one device may be relied on, other than what follows from the above.
Results may differ from a plain program's by a relative error of at most 0.017.
Values may be sent and summed in bfloat16 or wider, within the bound.
A program may use at most 64 MiB of HBM per device.

v0:
```python
import math
import jax
import jax.numpy as jnp
from jax import lax
from jax.sharding import PartitionSpec as P

E = 2048


def contract(left, right, left_dim, right_dim):
    return lax.dot_general(
        left, right, (((left_dim,), (right_dim,)), ((), ())), preferred_element_type=jnp.float32
    )


def local(programs, tests, weight, labels):
    factor = 1.0 / math.sqrt(E)
    targets = labels.astype(jnp.float32)
    w_rows = lax.all_gather(weight, "row", axis=1, tiled=True)
    share = lax.psum_scatter(
        jnp.dot(programs, w_rows, preferred_element_type=jnp.float32).astype(jnp.bfloat16),
        "col",
        scatter_dimension=0,
        tiled=True,
    )
    projected = lax.all_gather(share, "col", axis=0, tiled=True)
    test_whole = lax.all_gather(tests, "row", axis=1, tiled=True)
    logits = contract(projected, test_whole, 1, 1) * factor
    dlogits = (jax.nn.sigmoid(logits) - targets).astype(jnp.bfloat16)
    partial_sums = jnp.dot(dlogits, test_whole, preferred_element_type=jnp.float32)
    summed = lax.psum(partial_sums.astype(jnp.bfloat16), "col")
    grad_programs = (contract(summed, w_rows, 1, 1) * factor).astype(jnp.bfloat16)
    weight_part = contract(programs, summed, 0, 0) * factor
    test_part = contract(dlogits, projected, 0, 0) * factor
    grad_weight, test_total = (
        lax.psum_scatter(
            weight_part.astype(jnp.bfloat16), "row", scatter_dimension=1, tiled=True
        ).astype(jnp.float32),
        lax.psum_scatter(
            test_part.astype(jnp.bfloat16), "row", scatter_dimension=1, tiled=True
        ).astype(jnp.float32),
    )
    grad_tests = test_total.astype(jnp.bfloat16)
    return (grad_programs, grad_tests, grad_weight)


def solution(mesh):
    placed = (
        P(("grp", "row"), "col"),
        P(("grp", "col"), "row"),
        P("col", "row"),
        P(("grp", "row"), "col"),
    )
    return jax.shard_map(
        local,
        mesh=mesh,
        in_specs=placed,
        out_specs=(P(("grp", "row"), "col"), P(("grp", "col"), "row"), P(("grp", "col"), "row")),
        check_vma=False,
    )
```

profile of v0, /device:TPU:0, one launch (start us, length us, event | category | flops | bytes accessed | tf_op | source)
XLA Modules:
  0.0 236.3 jit_solution(9814701826729110321)
XLA Ops:
  7.2 0.0 copy-start
  7.2 0.0 all-gather.4.cloned.1.call-start
  7.2 0.7 all-gather.4.cloned.1.call-update
  7.9 0.0 reduce-scatter.4.cloned.1.call-start
  8.0 26.9 %all-gather.4.cloned.1.call-done = bf16[512,2048]{1,0:T(8,128)(2,1)} async-done(((bf16[512,512]{1,0:T(8,128)(2,1)}), bf16[512,2048]{1,0:T(8,128)(2,1)}) %all-gather.4.cloned.1.call-update) | async-done | bytes 2097168 | tf_op jit(solution)/shard_map/all_gather | solution.py:19
  34.9 3.3 %convolution_convert_fusion = bf16[256,2048]{1,0:T(8,128)(2,1)} fusion(bf16[256,512]{1,0:T(8,128)(2,1)S(1)} %copy-done, bf16[512,2048]{1,0:T(8,128)(2,1)} %all-gather.4.cloned.1.call-done), kind=kOutput, calls=%fused_computation.3 | convolution fusion | flops 537395200 | bytes 3407872 | tf_op jit(solution)/shard_map/dot_general | solution.py:21
  38.2 0.0 reduce-scatter.4.cloned.1.call-update
  38.2 0.0 all-gather.8.cloned.1.call-start
  38.2 0.7 all-gather.8.cloned.1.call-update
  38.9 0.0 all-gather.6.cloned.1.call-start
  39.0 26.5 %reduce-scatter.4.cloned.1.call-done = bf16[64,2048]{1,0:T(8,128)(2,1)} async-done(((bf16[256,2048]{1,0:T(8,128)(2,1)}), bf16[64,2048]{1,0:T(8,128)(2,1)}) %reduce-scatter.4.cloned.1.call-update) | async-done | bytes 262160 | tf_op jit(solution)/shard_map/reduce_scatter | solution.py:20
  65.5 0.0 all-gather.6.cloned.1.call-update
  65.5 0.0 all-reduce.2.cloned.1.call-start
  65.6 17.0 %all-gather.8.cloned.1.call-done = bf16[256,2048]{1,0:T(8,128)(2,1)} async-done(((bf16[256,512]{1,0:T(8,128)(2,1)}), bf16[256,2048]{1,0:T(8,128)(2,1)}) %all-gather.8.cloned.1.call-update) | async-done | bytes 1048592 | tf_op jit(solution)/shard_map/all_gather | solution.py:27
  82.6 29.5 %all-gather.6.cloned.1.call-done = bf16[256,2048]{1,0:T(8,128)(2,1)} async-done(((bf16[64,2048]{1,0:T(8,128)(2,1)}), bf16[256,2048]{1,0:T(8,128)(2,1)}) %all-gather.6.cloned.1.call-update) | async-done | bytes 1048592 | tf_op jit(solution)/shard_map/all_gather | solution.py:26
  112.0 0.0 copy-done.4
  112.0 2.0 fusion.8
  114.1 0.0 copy-done.3
  114.1 1.4 convolution_convert_fusion.1
  115.5 0.0 all-reduce.2.cloned.1.call-update
  115.5 0.0 reduce-scatter.8.cloned.1.call-start
  115.6 51.4 %all-reduce.2.cloned.1.call-done = bf16[256,2048]{1,0:T(8,128)(2,1)} async-done(((bf16[256,2048]{1,0:T(8,128)(2,1)}), bf16[256,2048]{1,0:T(8,128)(2,1)}) %all-reduce.2.cloned.1.call-update) | async-done | bytes 1048592 | tf_op jit(solution)/shard_map/psum | solution.py:31
  167.0 3.3 %fusion = bf16[512,2048]{0,1:T(8,128)(2,1)} fusion(bf16[256,2048]{1,0:T(8,128)(2,1)} %all-reduce.2.cloned.1.call-done, bf16[256,512]{1,0:T(8,128)(2,1)S(1)} %copy-done), kind=kOutput, calls=%fused_computation.1 | convolution fusion | flops 538968064 | bytes 3407872 | tf_op jit(solution)/shard_map/dot_general | solution.py:11
  170.3 0.0 reduce-scatter.8.cloned.1.call-update
  170.3 0.0 reduce-scatter.6.cloned.1.call-start
  170.4 1.1 copy-done.2
  171.5 1.4 fusion.1
  172.9 0.0 reduce-scatter.6.cloned.1.call-update
  173.0 2.7 %fusion.2 = bf16[256,512]{1,0:T(8,128)(2,1)} fusion(bf16[256,2048]{1,0:T(8,128)(2,1)} %all-reduce.2.cloned.1.call-done, bf16[512,2048]{1,0:T(8,128)(2,1)S(1)} %copy-done.1), kind=kOutput, calls=%fused_computation.7 | convolution fusion | flops 537133056 | bytes 3407872 | tf_op jit(solution)/shard_map/dot_general | solution.py:11
  175.6 25.6 %reduce-scatter.8.cloned.1.call-done = bf16[512,512]{0,1:T(8,128)(2,1)} async-done(((bf16[512,2048]{0,1:T(8,128)(2,1)}), bf16[512,512]{0,1:T(8,128)(2,1)}) %reduce-scatter.8.cloned.1.call-update) | async-done | bytes 524304 | tf_op jit(solution)/shard_map/reduce_scatter | solution.py:36
  201.3 2.2 copy.7
  203.5 25.9 %reduce-scatter.6.cloned.1.call-done = bf16[256,512]{1,0:T(8,128)(2,1)} async-done(((bf16[256,2048]{1,0:T(8,128)(2,1)}), bf16[256,512]{1,0:T(8,128)(2,1)}) %reduce-scatter.6.cloned.1.call-update) | async-done | bytes 262160 | tf_op jit(solution)/shard_map/reduce_scatter | solution.py:39
  (6 shorter events, 0.0 us)
Async XLA Ops:
  7.2 27.7 %copy-start = (bf16[256,512]{1,0:T(8,128)(2,1)S(1)}, bf16[256,512]{1,0:T(8,128)(2,1)}, u32[]{:S(2)}) copy-start(bf16[256,512]{1,0:T(8,128)(2,1)} %param.4) | copy-start | bytes 786436
  7.2 27.7 %all-gather.4.cloned.1.call-start = ((), (), s32[]{:S(2)}) async-start(), calls=%async_computation.3 | async-start | bytes 2621440 | tf_op jit(solution)/shard_map/all_gather | solution.py:19
  7.9 104.1 %copy-start.4 = (s32[256,256]{1,0:T(8,128)S(1)}, s32[256,256]{1,0:T(8,128)}, u32[]{:S(2)}) copy-start(s32[256,256]{1,0:T(8,128)} %param.7) | copy-start | bytes 786436
  7.9 57.6 %reduce-scatter.4.cloned.1.call-start = ((), (), s32[]{:S(2)}) async-start(), calls=%async_computation.4 | async-start | bytes 1310720 | tf_op jit(solution)/shard_map/reduce_scatter | solution.py:20
  38.2 44.4 %all-gather.8.cloned.1.call-start = ((), (), s32[]{:S(2)}) async-start(), calls=%async_computation.6 | async-start | bytes 1310720 | tf_op jit(solution)/shard_map/all_gather | solution.py:27
  38.9 73.1 %all-gather.6.cloned.1.call-start = ((), (), s32[]{:S(2)}) async-start(), calls=%async_computation.5 | async-start | bytes 1310720 | tf_op jit(solution)/shard_map/all_gather | solution.py:26
  65.5 101.5 %all-reduce.2.cloned.1.call-start = ((), (), s32[]{:S(2)}) async-start(), calls=%async_computation.7 | async-start | bytes 2097152 | tf_op jit(solution)/shard_map/psum | solution.py:31
  82.5 31.5 %copy-start.3 = (bf16[256,2048]{1,0:T(8,128)(2,1)S(1)}, bf16[256,2048]{1,0:T(8,128)(2,1)}, u32[]{:S(2)}) copy-start(bf16[256,2048]{1,0:T(8,128)(2,1)} %all-gather.8.cloned.1.call-done) | copy-start | bytes 3145732
  115.5 85.7 %reduce-scatter.8.cloned.1.call-start = ((), (), s32[]{:S(2)}) async-start(), calls=%async_computation.9 | async-start | bytes 2621440 | tf_op jit(solution)/shard_map/reduce_scatter | solution.py:36
  170.3 1.2 copy-start.2
  170.3 2.7 %copy-start.1 = (bf16[512,2048]{1,0:T(8,128)(2,1)S(1)}, bf16[512,2048]{1,0:T(8,128)(2,1)}, u32[]{:S(2)}) copy-start(bf16[512,2048]{1,0:T(8,128)(2,1)} %all-gather.4.cloned.1.call-done) | copy-start | bytes 6291460
  170.3 59.1 %reduce-scatter.6.cloned.1.call-start = ((), (), s32[]{:S(2)}) async-start(), calls=%async_computation.8 | async-start | bytes 1310720 | tf_op jit(solution)/shard_map/reduce_scatter | solution.py:39
Sparse Core Ops, SparseCore 0:
  9.6 25.2 all-gather.3
  38.3 27.1 reduce-scatter.3
  67.1 15.3 all-gather.7
  84.1 27.9 all-gather.5
  115.6 51.3 all-reduce.1
  170.4 30.7 reduce-scatter.7
  204.5 24.8 reduce-scatter.5
where the time goes:
time: 237 us; the launch traced here: 236 us
  waiting for transfers between devices  204 us (86%)
  between operations  14.2 us (6%)
  matrix products  14.1 us (6%)
  local copies, waits for them, and re-layouts  3.38 us (1%)
    psum x1, waiting for transfers between devices, local(): summed = lax.psum(partial_sums.astype(jnp.bfloat16), 'col')  51.4 us
    all_gather x1, waiting for transfers between devices, local(): projected = lax.all_gather(share, 'col', axis=0, tiled=True)  29.5 us
    all_gather x1, waiting for transfers between devices, local(): w_rows = lax.all_gather(weight, 'row', axis=1, tiled=True)  26.9 us
    reduce_scatter x1, waiting for transfers between devices, local(): lax.psum_scatter(jnp.dot(programs, w_rows, preferred_element_type=jnp.flo...  26.5 us
    reduce_scatter x1, waiting for transfers between devices, local(): lax.psum_scatter(test_part.astype(jnp.bfloat16), 'row', scatter_dimension...  25.9 us
    reduce_scatter x1, waiting for transfers between devices, local(): lax.psum_scatter(weight_part.astype(jnp.bfloat16), 'row', scatter_dimensi...  25.6 us
    all_gather x1, waiting for transfers between devices, local(): test_whole = lax.all_gather(tests, 'row', axis=1, tiled=True)  17 us
    dot_general x4, matrix products, contract(): lax.dot_general(left, right, (((left_dim,), (right_dim,)), ((), ())), pre...  9.44 us
  transfers between devices with their start and end apart: 7, of which 7 were waited for; matrix products, arithmetic and copies ran while one was open for 3% of the time, Pallas kernels for 0%

commit v1 on v0

--- a/solution.py
+++ b/solution.py
@@ -5,6 +5,7 @@
 from jax.sharding import PartitionSpec as P
 
 E = 2048
+shelves_run = lambda values: jnp.sum(jax.lax.all_gather(values, "col"), 0)
 
 
 def contract(left, right, left_dim, right_dim):
@@ -28,7 +29,7 @@
     logits = contract(projected, test_whole, 1, 1) * factor
     dlogits = (jax.nn.sigmoid(logits) - targets).astype(jnp.bfloat16)
     partial_sums = jnp.dot(dlogits, test_whole, preferred_element_type=jnp.float32)
-    summed = lax.psum(partial_sums.astype(jnp.bfloat16), "col")
+    summed = shelves_run(partial_sums.astype(jnp.bfloat16))
     grad_programs = (contract(summed, w_rows, 1, 1) * factor).astype(jnp.bfloat16)
     weight_part = contract(programs, summed, 0, 0) * factor
     test_part = contract(dlogits, projected, 0, 0) * factor

time: 237 us -> 266 us (1.12)
  waiting for transfers between devices: 204 us -> 232 us
  other arithmetic: 0 us -> 3.07 us
    all_gather x0 -> x1, waiting for transfers between devices: none -> 80.4 us  [shelves_run = lambda values: jnp.sum(jax.lax.all_gather(values, 'col'), 0)]
    psum x1 -> x0, waiting for transfers between devices: 51.4 us -> none  [local(): summed = lax.psum(partial_sums.astype(jnp.bfloat16), 'col')]
    reduce_sum x0 -> x1, other arithmetic: none -> 3.07 us  [shelves_run = lambda values: jnp.sum(jax.lax.all_gather(values, 'col'), 0)]
  transfers between devices with their start and end apart: 7 -> 7, of which waited for: 7 -> 7; matrix products, arithmetic and copies ran while one was open for 3% -> 2% of each run, Pallas kernels for 0% -> 0%
where the time goes in v1:
time: 266 us
  waiting for transfers between devices  232 us (87%)
  between operations  14.2 us (5%)
  matrix products  12.9 us (5%)
  local copies, waits for them, and re-layouts  3.39 us (1%)
  other arithmetic  3.07 us (1%)
    all_gather x1, waiting for transfers between devices, shelves_run = lambda values: jnp.sum(jax.lax.all_gather(values, 'col'), 0)  80.4 us
    all_gather x1, waiting for transfers between devices, local(): projected = lax.all_gather(share, 'col', axis=0, tiled=True)  29.5 us
    all_gather x1, waiting for transfers between devices, local(): w_rows = lax.all_gather(weight, 'row', axis=1, tiled=True)  26.9 us
    reduce_scatter x1, waiting for transfers between devices, local(): lax.psum_scatter(jnp.dot(programs, w_rows, preferred_element_type=jnp.flo...  26.5 us
    reduce_scatter x1, waiting for transfers between devices, local(): lax.psum_scatter(test_part.astype(jnp.bfloat16), 'row', scatter_dimension...  25.8 us
    reduce_scatter x1, waiting for transfers between devices, local(): lax.psum_scatter(weight_part.astype(jnp.bfloat16), 'row', scatter_dimensi...  24.8 us
    all_gather x1, waiting for transfers between devices, local(): test_whole = lax.all_gather(tests, 'row', axis=1, tiled=True)  17 us
    dot_general x4, matrix products, contract(): lax.dot_general(left, right, (((left_dim,), (right_dim,)), ((), ())), pre...  8.23 us
  transfers between devices with their start and end apart: 7, of which 7 were waited for; matrix products, arithmetic and copies ran while one was open for 2% of the time, Pallas kernels for 0%

profile of v1, /device:TPU:0, one launch (start us, length us, event | category | flops | bytes accessed | tf_op | source)
XLA Modules:
  0.0 266.1 jit_solution(17108373840968696507)
XLA Ops:
  7.2 0.0 copy-start
  7.2 0.0 all-gather.6.cloned.1.call-start
  7.2 0.7 all-gather.6.cloned.1.call-update
  7.9 0.0 reduce-scatter.4.cloned.1.call-start
  8.0 26.9 %all-gather.6.cloned.1.call-done = bf16[512,2048]{1,0:T(8,128)(2,1)} async-done(((bf16[512,512]{1,0:T(8,128)(2,1)}), bf16[512,2048]{1,0:T(8,128)(2,1)}) %all-gather.6.cloned.1.call-update) | async-done | bytes 2097168 | tf_op jit(solution)/shard_map/all_gather | solution.py:20
  34.9 3.3 %convolution_convert_fusion = bf16[256,2048]{1,0:T(8,128)(2,1)} fusion(bf16[256,512]{1,0:T(8,128)(2,1)S(1)} %copy-done, bf16[512,2048]{1,0:T(8,128)(2,1)} %all-gather.6.cloned.1.call-done), kind=kOutput, calls=%fused_computation.3 | convolution fusion | flops 537395200 | bytes 3407872 | tf_op jit(solution)/shard_map/dot_general | solution.py:22
  38.2 0.0 reduce-scatter.4.cloned.1.call-update
  38.2 0.0 all-gather.10.cloned.1.call-start
  38.2 0.7 all-gather.10.cloned.1.call-update
  38.9 0.0 all-gather.8.cloned.1.call-start
  39.0 26.5 %reduce-scatter.4.cloned.1.call-done = bf16[64,2048]{1,0:T(8,128)(2,1)} async-done(((bf16[256,2048]{1,0:T(8,128)(2,1)}), bf16[64,2048]{1,0:T(8,128)(2,1)}) %reduce-scatter.4.cloned.1.call-update) | async-done | bytes 262160 | tf_op jit(solution)/shard_map/reduce_scatter | solution.py:21
  65.5 0.0 all-gather.8.cloned.1.call-update
  65.5 0.0 all-gather.12.cloned.1.call-start
  65.6 17.0 %all-gather.10.cloned.1.call-done = bf16[256,2048]{1,0:T(8,128)(2,1)} async-done(((bf16[256,512]{1,0:T(8,128)(2,1)}), bf16[256,2048]{1,0:T(8,128)(2,1)}) %all-gather.10.cloned.1.call-update) | async-done | bytes 1048592 | tf_op jit(solution)/shard_map/all_gather | solution.py:28
  82.6 29.5 %all-gather.8.cloned.1.call-done = bf16[256,2048]{1,0:T(8,128)(2,1)} async-done(((bf16[64,2048]{1,0:T(8,128)(2,1)}), bf16[256,2048]{1,0:T(8,128)(2,1)}) %all-gather.8.cloned.1.call-update) | async-done | bytes 1048592 | tf_op jit(solution)/shard_map/all_gather | solution.py:27
  112.0 2.0 fusion.8
  114.1 1.4 convolution_convert_fusion.1
  115.5 0.0 all-gather.12.cloned.1.call-update
  115.5 0.0 reduce-scatter.8.cloned.1.call-start
  115.6 80.4 %all-gather.12.cloned.1.call-done = bf16[1024,2048]{1,0:T(8,128)(2,1)} async-done(((bf16[256,2048]{1,0:T(8,128)(2,1)}), bf16[1024,2048]{1,0:T(8,128)(2,1)}) %all-gather.12.cloned.1.call-update) | async-done | bytes 4194320 | tf_op jit(solution)/shard_map/all_gather | solution.py:8
  195.9 3.1 %reduce_sum.12 = bf16[256,2048]{1,0:T(8,128)(2,1)S(1)} reduce(bf16[4,256,2048]{2,1,0:T(8,128)(2,1)} %bitcast.15, bf16[]{:T(256)} %constant.5.clone.1), dimensions={0}, to_apply=%region_1.0 | reduce | flops 1572864 | bytes 5242882 | tf_op jit(solution)/shard_map/reduce_sum | solution.py:8
  199.0 0.0 copy-start.4
  199.0 2.1 fusion
  201.1 0.0 reduce-scatter.8.cloned.1.call-update
  201.1 0.0 reduce-scatter.6.cloned.1.call-start
  201.2 1.1 copy-done.2
  202.3 1.4 fusion.1
  203.7 0.0 reduce-scatter.6.cloned.1.call-update
  203.8 2.7 %fusion.2 = bf16[256,512]{1,0:T(8,128)(2,1)} fusion(bf16[256,2048]{1,0:T(8,128)(2,1)} %copy-done.4, bf16[512,2048]{1,0:T(8,128)(2,1)S(1)} %copy-done.1), kind=kOutput, calls=%fused_computation.7 | convolution fusion | flops 537133056 | bytes 3407872 | tf_op jit(solution)/shard_map/dot_general | solution.py:12
  206.5 24.8 %reduce-scatter.8.cloned.1.call-done = bf16[512,512]{0,1:T(8,128)(2,1)} async-done(((bf16[512,2048]{0,1:T(8,128)(2,1)}), bf16[512,512]{0,1:T(8,128)(2,1)}) %reduce-scatter.8.cloned.1.call-update) | async-done | bytes 524304 | tf_op jit(solution)/shard_map/reduce_scatter | solution.py:37
  231.2 2.2 copy.7
  233.4 25.8 %reduce-scatter.6.cloned.1.call-done = bf16[256,512]{1,0:T(8,128)(2,1)} async-done(((bf16[256,2048]{1,0:T(8,128)(2,1)}), bf16[256,512]{1,0:T(8,128)(2,1)}) %reduce-scatter.6.cloned.1.call-update) | async-done | bytes 262160 | tf_op jit(solution)/shard_map/reduce_scatter | solution.py:40
  (9 shorter events, 0.0 us)
Async XLA Ops:
  7.2 27.7 %copy-start = (bf16[256,512]{1,0:T(8,128)(2,1)S(1)}, bf16[256,512]{1,0:T(8,128)(2,1)}, u32[]{:S(2)}) copy-start(bf16[256,512]{1,0:T(8,128)(2,1)} %param.4) | copy-start | bytes 786436
  7.2 27.7 %all-gather.6.cloned.1.call-start = ((), (), s32[]{:S(2)}) async-start(), calls=%async_computation.3 | async-start | bytes 2621440 | tf_op jit(solution)/shard_map/all_gather | solution.py:20
  7.9 104.1 %copy-start.5 = (s32[256,256]{1,0:T(8,128)S(1)}, s32[256,256]{1,0:T(8,128)}, u32[]{:S(2)}) copy-start(s32[256,256]{1,0:T(8,128)} %param.7) | copy-start | bytes 786436
  7.9 57.6 %reduce-scatter.4.cloned.1.call-start = ((), (), s32[]{:S(2)}) async-start(), calls=%async_computation.4 | async-start | bytes 1310720 | tf_op jit(solution)/shard_map/reduce_scatter | solution.py:21
  38.2 44.4 %all-gather.10.cloned.1.call-start = ((), (), s32[]{:S(2)}) async-start(), calls=%async_computation.6 | async-start | bytes 1310720 | tf_op jit(solution)/shard_map/all_gather | solution.py:28
  38.9 73.1 %all-gather.8.cloned.1.call-start = ((), (), s32[]{:S(2)}) async-start(), calls=%async_computation.5 | async-start | bytes 1310720 | tf_op jit(solution)/shard_map/all_gather | solution.py:27
  65.5 130.4 %all-gather.12.cloned.1.call-start = ((), (), s32[]{:S(2)}) async-start(), calls=%async_computation.9 | async-start | bytes 5242880 | tf_op jit(solution)/shard_map/all_gather | solution.py:8
  82.5 31.5 %copy-start.3 = (bf16[256,2048]{1,0:T(8,128)(2,1)S(1)}, bf16[256,2048]{1,0:T(8,128)(2,1)}, u32[]{:S(2)}) copy-start(bf16[256,2048]{1,0:T(8,128)(2,1)} %all-gather.10.cloned.1.call-done) | copy-start | bytes 3145732
  115.5 115.7 %reduce-scatter.8.cloned.1.call-start = ((), (), s32[]{:S(2)}) async-start(), calls=%async_computation.8 | async-start | bytes 2621440 | tf_op jit(solution)/shard_map/reduce_scatter | solution.py:37
  199.0 2.1 copy-start.4
  201.1 1.2 copy-start.2
  201.1 2.7 copy-start.1
  201.1 58.1 %reduce-scatter.6.cloned.1.call-start = ((), (), s32[]{:S(2)}) async-start(), calls=%async_computation.7 | async-start | bytes 1310720 | tf_op jit(solution)/shard_map/reduce_scatter | solution.py:40
Sparse Core Ops, SparseCore 0:
  9.6 25.2 all-gather.5
  38.3 27.1 reduce-scatter.3
  67.1 15.3 all-gather.9
  84.1 27.9 all-gather.7
  115.6 80.2 all-gather.11
  201.2 29.9 reduce-scatter.7
  234.3 24.8 reduce-scatter.5
